TPU v7x, 32 devices: a whole 2x2x4 slice. The times are simulated.
32 devices in a mesh: ctx: 16 (over z, x, core), head: 2 (over y).
Axes of the slice: x: 2, y: 2, z: 4, core: 2. Of those that a mesh axis runs over, the one named last changes fastest.
Arguments:
- query_rows: bfloat16 [8192, 2048], P('ctx', 'head'), may hold values from -60 to 60
- key_rows: bfloat16 [8192, 2048], P('ctx', 'head'), may hold values from -6 to 6
- value_rows: bfloat16 [8192, 2048], P('ctx', 'head'), may hold values from -60 to 60
- log_gate: float32 [16, 8192], P('head', 'ctx'), may hold values from -0.5 to 0
- conv_weight: float32 [3, 4, 2048], P(None, None, 'head'), may hold values from -3 to 3
- norm_gain: float32 [2048], P('head'), may hold values from 0.5 to 1.5
- mixed_grad: bfloat16 [8192, 2048], P('ctx', 'head'), may hold values from -24 to 24
Outputs:
- mixer_out: bfloat16 [8192, 2048], P('ctx', 'head')
- query_grad: bfloat16 [8192, 2048], P('ctx', 'head')
- key_grad: bfloat16 [8192, 2048], P('ctx', 'head')
- value_grad: bfloat16 [8192, 2048], P('ctx', 'head')
- conv_grad: float32 [3, 4, 2048], P(None, None, 'head')
- gain_grad: float32 [2048], P('head')
All inputs are finite; a program needn't handle non-finite values.
Results may differ from a plain program's by a relative error of at most 0.015.
Values may be sent and summed in bfloat16 or wider, within the bound.
A program may use at most 128 MiB of HBM per device.

v0:
```python
import jax
import jax.numpy as jnp
from jax import lax
from jax.sharding import PartitionSpec as P

HD = 128
TAPS = 4
GROUP = 512
D = 2048
norm_epsilon = 1e-05


def shifted(block, axis, distance):
    devices = range(lax.axis_size(axis))
    route = [(i - distance, i) for i in devices if i - distance in devices]
    return lax.ppermute(block, axis, route)


def prefix(value, axis, join, neutral):
    count = lax.axis_size(axis)
    place = lax.axis_index(axis)
    ahead = count - 1 - place
    gathered = jax.tree.map(
        lambda a, kind: lax.all_gather(a.astype(kind), axis), value, (jnp.bfloat16, jnp.bfloat16)
    )
    state = jax.tree.map(lambda a, e: jnp.zeros_like(a) + jnp.asarray(e, a.dtype), value, neutral)

    def one(turn, state):
        source = count - 1 - turn
        return join(
            state,
            jax.tree.map(
                lambda a, own: lax.dynamic_index_in_dim(a, source, 0, False).astype(own.dtype),
                gathered,
                value,
            ),
        )

    return lax.fori_loop(0, ahead, one, state)


def rounded(values):
    return values.astype(jnp.bfloat16)


def decay_tables(gate_blocks):
    running = jnp.cumsum(gate_blocks, axis=-1)
    closing = running[..., -1]
    gap_matrix = running[..., :, None] - running[..., None, :]
    block_size = gate_blocks.shape[-1]
    lower_mask = jnp.arange(block_size)[:, None] >= jnp.arange(block_size)[None, :]
    weights = jnp.where(lower_mask, jnp.exp(jnp.minimum(gap_matrix, 0.0)), 0.0)
    return (running, closing, weights)


def chain_step(earlier, later_part):
    return (
        earlier[0] + later_part[0],
        jnp.exp(later_part[0])[..., None, None] * earlier[1] + later_part[1],
    )


def local_chain(closing, blocks, backwards):

    def advance(partial_sum, block_item):
        return (chain_step(partial_sum, block_item), partial_sum)

    initial = (jnp.zeros(closing.shape[1:], jnp.float32), jnp.zeros(blocks.shape[1:], jnp.float32))
    return lax.scan(advance, initial, (closing, blocks), reverse=backwards)


def conv_forward(rim_rows, rows, weight, tok_here):
    extended = jnp.concatenate([rim_rows, rows], axis=0).astype(jnp.float32)
    result = weight[0][None, :] * extended[TAPS - 1 : TAPS - 1 + tok_here]
    for offset in range(1, TAPS):
        result = (
            result
            + weight[offset][None, :] * extended[TAPS - 1 - offset : TAPS - 1 - offset + tok_here]
        )
    return (rounded(result), extended)


def conv_backward(grad_rows, edge_rows, extended, weight, tok_here):
    ahead_all = jnp.concatenate([grad_rows, edge_rows], axis=0)
    input_grad = weight[0][None, :] * grad_rows
    weight_grad = [jnp.sum(grad_rows * extended[TAPS - 1 : TAPS - 1 + tok_here], axis=0)]
    for offset in range(1, TAPS):
        input_grad = input_grad + weight[offset][None, :] * ahead_all[offset : offset + tok_here]
        weight_grad.append(
            jnp.sum(grad_rows * extended[TAPS - 1 - offset : TAPS - 1 - offset + tok_here], axis=0)
        )
    return (rounded(input_grad), jnp.stack(weight_grad))


def body(query_rows, key_rows, value_rows, log_gate, conv_weight, norm_gain, mixed_grad):
    tok_here = query_rows.shape[0]
    width_here = query_rows.shape[1]
    heads_here = width_here // HD
    block_count = tok_here // GROUP
    rim_rows = shifted(
        jnp.stack(
            [
                query_rows[tok_here - (TAPS - 1) :],
                key_rows[tok_here - (TAPS - 1) :],
                value_rows[tok_here - (TAPS - 1) :],
            ]
        ),
        "ctx",
        1,
    )
    query_conv, query_ext = conv_forward(rim_rows[0], query_rows, conv_weight[0], tok_here)
    key_conv, key_ext = conv_forward(rim_rows[1], key_rows, conv_weight[1], tok_here)
    value_conv, value_ext = conv_forward(rim_rows[2], value_rows, conv_weight[2], tok_here)
    query_blocks = query_conv.reshape(block_count, GROUP, heads_here, HD)
    key_blocks = key_conv.reshape(block_count, GROUP, heads_here, HD)
    value_blocks = value_conv.reshape(block_count, GROUP, heads_here, HD)
    gate_blocks = log_gate.reshape(heads_here, block_count, GROUP).transpose(1, 0, 2)
    running, closing, weights = decay_tables(gate_blocks)
    grow_factor = jnp.exp(running).transpose(0, 2, 1)[..., None]
    shrink = jnp.exp(closing[..., None] - running).transpose(0, 2, 1)[..., None]
    scores = jnp.einsum(
        "nthd,nshd->nhts", query_blocks, key_blocks, preferred_element_type=jnp.float32
    )
    weights_low = rounded(scores * weights)
    key_scaled = rounded(key_blocks * shrink)
    blocks = jnp.einsum(
        "nshd,nshe->nhde", key_scaled, value_blocks, preferred_element_type=jnp.float32
    )
    device_sum, before = local_chain(closing, blocks, False)
    zero_state = jnp.zeros((heads_here, HD, HD), jnp.float32)
    all_totals = lax.all_gather(device_sum[0][None], "ctx", axis=0, tiled=True)
    device_index = lax.axis_index("ctx")
    cumulative = jnp.cumsum(all_totals, axis=0)
    before_me = cumulative[device_index] - all_totals[device_index]
    sources = jnp.arange(all_totals.shape[0])
    factor_table = jnp.where(
        (sources < device_index)[:, None],
        jnp.exp(jnp.minimum(before_me[None, :] - cumulative, 0.0)),
        0.0,
    )
    incoming = jnp.einsum(
        "nh,nhde->hde",
        factor_table,
        lax.all_gather(device_sum[1][None], "ctx", axis=0, tiled=True),
        precision=lax.Precision.HIGHEST,
    )
    group_in = jnp.exp(before[0])[..., None, None] * incoming[None] + before[1]
    state_low = rounded(group_in)
    attended = jnp.einsum(
        "nhts,nshe->nthe", weights_low, value_blocks, preferred_element_type=jnp.float32
    )
    attended = (
        attended
        + jnp.einsum("nthd,nhde->nthe", query_blocks, state_low, preferred_element_type=jnp.float32)
        * grow_factor
    )
    attended = attended.reshape(tok_here, width_here)
    grad_wide = mixed_grad.astype(jnp.float32)
    scaled = grad_wide * norm_gain[None, :]
    squares = lax.psum(jnp.sum(attended * attended, axis=1), "head")
    inverse = lax.rsqrt(squares / D + norm_epsilon)
    inner_sum = lax.psum(jnp.sum(scaled * attended, axis=1), "head") / D
    normed = attended * inverse[:, None]
    mixer_out = rounded(normed * norm_gain[None, :])
    gain_part = jnp.sum(grad_wide * normed, axis=0)
    out_grad = rounded(
        inverse[:, None] * (scaled - attended * (inverse * inverse * inner_sum)[:, None])
    )
    grad_blocks = out_grad.reshape(block_count, GROUP, heads_here, HD)
    grad_scores = rounded(
        jnp.einsum("nthe,nshe->nhts", grad_blocks, value_blocks, preferred_element_type=jnp.float32)
        * weights
    )
    query_scaled = rounded(query_blocks * grow_factor)
    back_blocks = jnp.einsum(
        "nthd,nthe->nhde", query_scaled, grad_blocks, preferred_element_type=jnp.float32
    )
    back_sum, back_before = local_chain(closing, back_blocks, True)
    later_state = prefix(
        (back_sum[0], back_sum[1]),
        "ctx",
        chain_step,
        (jnp.zeros((heads_here,), jnp.float32), zero_state),
    )[1]
    later_low = rounded(
        jnp.exp(back_before[0])[..., None, None] * later_state[None] + back_before[1]
    )
    query_cg = jnp.einsum(
        "nhts,nshd->nthd", grad_scores, key_blocks, preferred_element_type=jnp.float32
    )
    query_cg = (
        query_cg
        + jnp.einsum("nthe,nhde->nthd", grad_blocks, state_low, preferred_element_type=jnp.float32)
        * grow_factor
    )
    key_cg = jnp.einsum(
        "nhts,nthd->nshd", grad_scores, query_blocks, preferred_element_type=jnp.float32
    )
    key_cg = (
        key_cg
        + jnp.einsum("nshe,nhde->nshd", value_blocks, later_low, preferred_element_type=jnp.float32)
        * shrink
    )
    value_cg = jnp.einsum(
        "nhts,nthe->nshe", weights_low, grad_blocks, preferred_element_type=jnp.float32
    )
    value_cg = (
        value_cg
        + jnp.einsum("nshd,nhde->nshe", key_blocks, later_low, preferred_element_type=jnp.float32)
        * shrink
    )
    query_cg = query_cg.reshape(tok_here, width_here)
    key_cg = key_cg.reshape(tok_here, width_here)
    value_cg = value_cg.reshape(tok_here, width_here)
    edge_rows = shifted(
        jnp.stack([query_cg[: TAPS - 1], key_cg[: TAPS - 1], value_cg[: TAPS - 1]]), "ctx", -1
    )
    query_grad, query_taps = conv_backward(
        query_cg, edge_rows[0], query_ext, conv_weight[0], tok_here
    )
    key_grad, key_taps = conv_backward(key_cg, edge_rows[1], key_ext, conv_weight[1], tok_here)
    value_grad, value_taps = conv_backward(
        value_cg, edge_rows[2], value_ext, conv_weight[2], tok_here
    )
    conv_part = jnp.stack([query_taps, key_taps, value_taps])
    conv_grad, gain_grad = lax.psum((conv_part, gain_part), "ctx")
    return (mixer_out, query_grad, key_grad, value_grad, conv_grad, gain_grad)


def solution(mesh):
    placed = (
        P("ctx", "head"),
        P("ctx", "head"),
        P("ctx", "head"),
        P("head", "ctx"),
        P(None, None, "head"),
        P("head"),
        P("ctx", "head"),
    )
    return jax.shard_map(
        body,
        mesh=mesh,
        in_specs=placed,
        out_specs=(
            P("ctx", "head"),
            P("ctx", "head"),
            P("ctx", "head"),
            P("ctx", "head"),
            P(None, None, "head"),
            P("head"),
        ),
        check_vma=False,
    )
```

profile of v0, /device:TPU:0, one launch (start us, length us, event | category | flops | bytes accessed | tf_op | source)
XLA Modules:
  0.0 309.8 jit_solution(4000271757423066720)
XLA Ops:
  8.8 2.4 collective-permute-start
  11.2 2.2 reduce-window.6
  16.5 1.7 maximum_convert_fusion
  19.7 1.5 copy.163
  21.2 4.9 %fusion.49 = bf16[64,8,8,128]{3,2,1,0:T(8,128)(2,1)S(1)} fusion(f32[515,1024]{1,0:T(8,128)} %maximum_convert_fusion, f32[1024]{0:T(1024)S(1)} %bitcast.226, f32[1024]{0:T(1024)S(1)} %bitcast.228, f32[1024]{0:T(1024)S(1)} %bitcast.230, f32[1024]{0:T(1024)S(1)} %bitcast.224), kind=kLoop, calls=%fused_computation.94 | loop fusion | flops 4194304 | bytes 9453568
  26.1 1.3 convolution_add_fusion.1
  28.5 22.8 %all-gather = f32[16,8,1]{1,2,0:T(1,128)S(1)} all-gather(f32[1,8,1]{1,2,0:T(1,128)S(1)} %get-tuple-element.187), channel_id=2, replica_groups=mesh['ctx'=16,'head'=2] {'ctx'}, dimensions={0}, use_global_device_ids=true | all-gather | bytes 544 | tf_op jit(solution)/shard_map/all_gather | solution.py:131
  52.4 1.4 bitcast_add_fusion
  53.7 1.5 maximum_convert_fusion.1
  55.3 1.3 copy-done
  56.6 1.9 add_convert_fusion.1
  58.5 2.3 copy.213
  62.0 2.9 multiply_convert_fusion.1
  65.0 2.0 copy-done.2
  66.9 2.8 fusion.42
  69.8 35.3 %all-gather.7.cloned.1.call-done = f32[128,128,128]{2,1,0:T(8,128)} async-done(((f32[8,128,128]{2,1,0:T(8,128)}), f32[128,128,128]{2,1,0:T(8,128)}) %all-gather.7.cloned.1.call-update) | async-done | bytes 8388624 | tf_op jit(solution)/shard_map/all_gather | solution.py:144
  105.1 12.5 %fusion = f32[8,1,128,128]{3,1,2,0:T(1,128)S(1)} fusion(f32[16,8,1,1]{0,2,3,1:T(1,128)S(1)} %copy.206, f32[16,8,128,128]{3,2,1,0:T(8,128)} %bitcast.188), kind=kOutput, calls=%fused_computation.2 | convolution fusion | flops 25165824 | bytes 8913408 | tf_op jit(solution)/shard_map/nh,nhde->hde/dot_general | solution.py:141
  117.6 1.9 multiply_reduce_fusion.12
  119.5 5.1 %psum.28 = f32[512]{0:T(512)S(1)} all-reduce(f32[512]{0:T(512)S(1)} %get-tuple-element.206), channel_id=1, replica_groups=mesh['ctx'=16,'head'=2] {'head'}, use_global_device_ids=true, to_apply=%region_4.5 | all-reduce | flops 512 | bytes 4096 | tf_op jit(solution)/shard_map/psum | solution.py:160
  124.7 2.9 copy.169
  127.6 2.6 fusion.7
  130.2 4.9 %psum.29 = f32[512]{0:T(512)S(1)} all-reduce(f32[512]{0:T(512)S(1)} %get-tuple-element.166), channel_id=1, replica_groups=mesh['ctx'=16,'head'=2] {'head'}, use_global_device_ids=true, to_apply=%region_6.7 | all-reduce | flops 512 | bytes 4096 | tf_op jit(solution)/shard_map/psum | solution.py:162
  135.2 3.9 %fusion.6 = (bf16[512,1024]{1,0:T(8,128)(2,1)}, bf16[512,1024]{1,0:T(8,128)(2,1)}) fusion(bf16[512,1024]{1,0:T(8,128)(2,1)} %param.15, f32[512,1024]{1,0:T(8,128)} %copy.169, f32[512]{0:T(512)S(1)} %multiply_multiply_fusion, f32[1024]{0:T(1024)S(1)} %copy-done.25, f32[512]{0:T(512)S(1)} %add_rsqrt_fusion), kind=kLoop, calls=%fused_computation.19 | loop fusion | flops 4718592 | bytes 5251072 | tf_op jit(solution)/shard_map/convert_element_type | solution.py:43
  139.0 2.3 copy.214
  141.3 2.7 fusion.39
  144.0 18.6 %all-gather.3 = bf16[16,8,1]{1,2,0:T(2,128)(2,1)S(1)} all-gather(bf16[1,8,1]{1,2,0:T(2,128)(2,1)S(1)} %slice.396), channel_id=5, replica_groups=mesh['ctx'=16,'head'=2] {'ctx'}, dimensions={0}, use_global_device_ids=true | all-gather | bytes 272 | tf_op jit(solution)/shard_map/all_gather | solution.py:24
  162.7 4.0 %multiply_convert_fusion = bf16[8,512,512]{2,1,0:T(8,128)(2,1)S(1)} fusion(f32[8,512]{1,0:T(8,128)S(1)} %copy-done.27, pred[512,512]{1,0:T(8,128)(4,1)} %iota_compare_fusion, bf16[512,8,128]{0,2,1:T(8,128)(2,1)} %bitcast.185, bf16[64,8,8,128]{3,2,1,0:T(8,128)(2,1)S(1)} %fusion.49), kind=kOutput, calls=%fused_computation.4 | convolution fusion | flops 547356672 | bytes 6569984 | tf_op jit(solution)/shard_map/nthe,nshe->nhts/dot_general | solution.py:171
  166.7 1.5 fusion.62
  169.7 1.3 copy-done.5
  171.9 1.2 copy.186
  173.1 4.4 %fusion.64 = f32[8,128,512]{2,1,0:T(8,128)} fusion(bf16[512,8,128]{0,2,1:T(8,128)(2,1)S(1)} %bitcast.187, bf16[8,512,512]{2,1,0:T(8,128)(2,1)} %copy-done.2), kind=kOutput, calls=%fused_computation.139 | convolution fusion | flops 536870912 | bytes 7340032 | tf_op jit(solution)/shard_map/nhts,nthe->nshe/dot_general | solution.py:204
  177.5 2.0 fusion.63
  179.6 13.5 %all-gather.9.cloned.1.call-done = bf16[128,128,128]{2,1,0:T(8,128)(2,1)} async-done(((bf16[8,128,128]{2,1,0:T(8,128)(2,1)}), bf16[128,128,128]{2,1,0:T(8,128)(2,1)}) %all-gather.9.cloned.1.call-update) | async-done | bytes 4194320 | tf_op jit(solution)/shard_map/all_gather | solution.py:24
  193.1 17.3 %while.9 = (s32[]{:T(128)}, f32[8,128,128]{2,1,0:T(8,128)S(1)}, s32[]{:T(128)}, bf16[16,8]{1,0:T(8,128)(2,1)S(1)}, bf16[16,8,128,128]{3,2,1,0:T(8,128)(2,1)}, /*index=5*/s32[]{:T(128)}, s32[]{:T(128)}, s32[]{:T(128)}, s32[]{:T(128)}) while((s32[]{:T(128)}, f32[8,128,128]{2,1,0:T(8,128)S(1)}, s32[]{:T(128)}, bf16[16,8]{1,0:T(8,128)(2,1)S(1)}, ...), condition=%wide.region_8.9_spmd, body=%wide.region_7.8_spmd.sunk | while | flops 393230 | bytes 1310955 | solution.py:39
  193.2 1.1 convert_add_fusion.2
  196.6 1.1 convert_add_fusion.2
  210.4 2.4 fusion.35
  212.9 1.3 copy-done.6
  214.4 2.4 fusion.36
  216.8 1.3 copy-done.7
  218.4 1.6 collective-permute-start.1
  220.0 3.0 copy.176
  222.9 2.9 copy.192
  225.9 2.9 copy.190
  228.8 8.9 %multiply_reduce_fusion.3 = (f32[1024]{0:T(1024)S(1)}, f32[1024]{0:T(1024)S(1)}, f32[1024]{0:T(1024)S(1)}, f32[1024]{0:T(1024)S(1)}, bf16[512,1024]{1,0:T(8,128)(2,1)}) fusion(f32[512,1024]{1,0:T(8,128)} %copy.192, f32[515,1024]{1,0:T(8,128)} %maximum_convert_fusion, f32[3,1024]{1,0:T(4,128)S(1)} %get-tuple-element.188, f32[1024]{0:T(1024)S(1)} %bitcast.227, ...), kind=kLoop, calls=%fused_computation.62 | loop fusion | flops 9957376 | bytes 11579392 | tf_op jit(solution)/shard_map/reduce_sum | solution.py:86
  237.7 2.9 multiply_reduce_fusion.11
  240.6 2.9 multiply_reduce_fusion.7
  243.7 59.3 %all-reduce = (f32[3,4,1024]{2,1,0:T(4,128)}, f32[1024]{0:T(1024)}) all-reduce(f32[3,4,1024]{2,1,0:T(4,128)S(1)} %pad_maximum_fusion.4, f32[1024]{0:T(1024)S(1)} %get-tuple-element.165), channel_id=1, replica_groups=mesh['ctx'=16,'head'=2] {'ctx'}, use_global_device_ids=true, to_apply=%region_21.22 | all-reduce | flops 13312 | bytes 106496 | tf_op jit(solution)/shard_map/psum | solution.py:226
  (133 shorter events, 27.2 us)
Async XLA Ops:
  7.2 9.3 %copy-start.21 = (bf16[512,1024]{1,0:T(8,128)(2,1)S(1)}, bf16[512,1024]{1,0:T(8,128)(2,1)}, u32[]{:S(2)}) copy-start(bf16[512,1024]{1,0:T(8,128)(2,1)} %param.11) | copy-start | bytes 3145732
  7.2 97.9 %all-gather.7.cloned.1.call-start = ((), (), s32[]{:S(2)}) async-start(), calls=%async_computation | async-start | bytes 8912896 | tf_op jit(solution)/shard_map/all_gather | solution.py:144
  8.8 7.1 %collective-permute-start = (bf16[3,3,1024]{2,1,0:T(4,128)(2,1)S(1)}, bf16[3,3,1024]{2,1,0:T(4,128)(2,1)S(1)}, u32[]{:S(2)}, u32[]{:S(2)}) collective-permute-start(bf16[3,3,1024]{2,1,0:T(4,128)(2,1)S(1)} %pad_maximum_fusion.5), channel_id=1, source_target_pairs={{0,2},{2,4},{4,6},{6,8},{8,10},{10,12},{12,14},{14,16},{16,18},{18... | collective-permute-start | bytes 55304 | tf_op jit(solution)/shard_map/ppermute | solution.py:16
  13.6 2.1 copy-start.24
  15.7 2.5 copy-start.22
  15.8 10.3 %copy-start.28 = (f32[8]{0:T(128)}, f32[8]{0:T(128)S(1)}, u32[]{:S(2)}) copy-start(f32[8]{0:T(128)S(1)} %exponential_multiply_fusion) | copy-start | bytes 100
  21.2 4.9 %copy-start.18 = (bf16[512,8,128]{0,2,1:T(8,128)(2,1)S(1)}, bf16[512,8,128]{0,2,1:T(8,128)(2,1)}, u32[]{:S(2)}) copy-start(bf16[512,8,128]{0,2,1:T(8,128)(2,1)} %copy.163) | copy-start | bytes 3145732
  26.1 136.6 %copy-start.8 = (bf16[64,8,8,128]{3,2,1,0:T(8,128)(2,1)}, bf16[64,8,8,128]{3,2,1,0:T(8,128)(2,1)S(1)}, u32[]{:S(2)}) copy-start(bf16[64,8,8,128]{3,2,1,0:T(8,128)(2,1)S(1)} %fusion.49) | copy-start | bytes 3145732
  27.4 165.6 %all-gather.9.cloned.1.call-start = ((), (), s32[]{:S(2)}) async-start(), calls=%async_computation.1 | async-start | bytes 4456448 | tf_op jit(solution)/shard_map/all_gather | solution.py:24
  55.2 1.3 copy-start
  60.7 1.2 copy-start.9
  60.7 1.3 copy-start.23
  60.8 1.3 copy-start.26
  61.7 3.2 %copy-start.20 = (bf16[64,8,8,128]{3,2,1,0:T(8,128)(2,1)}, bf16[64,8,8,128]{3,2,1,0:T(8,128)(2,1)S(1)}, u32[]{:S(2)}) copy-start(bf16[64,8,8,128]{3,2,1,0:T(8,128)(2,1)S(1)} %fusion.78) | copy-start | bytes 3145732
  65.0 2.0 copy-start.2
  105.1 12.5 %copy-start.10 = (bf16[512,1024]{0,1:T(8,128)(2,1)S(1)}, bf16[512,1024]{0,1:T(8,128)(2,1)}, u32[]{:S(2)}) copy-start(bf16[512,1024]{0,1:T(8,128)(2,1)} %copy.213) | copy-start | bytes 3145732
  105.1 12.5 %copy-start.13 = (f32[8,128,512]{2,1,0:T(8,128)S(1)}, f32[8,128,512]{2,1,0:T(8,128)}, u32[]{:S(2)}) copy-start(f32[8,128,512]{2,1,0:T(8,128)} %fusion.42) | copy-start | bytes 6291460
  117.6 1.9 copy-start.16
  124.7 2.9 copy-start.25
  139.0 2.3 copy-start.29
  139.0 23.6 %copy-start.27 = (f32[8,512]{1,0:T(8,128)S(1)}, f32[8,512]{1,0:T(8,128)}, u32[]{:S(2)}) copy-start(f32[8,512]{1,0:T(8,128)} %bitcast_add_fusion) | copy-start | bytes 49156
  162.7 4.1 %copy-start.19 = (bf16[512,8,128]{0,2,1:T(8,128)(2,1)S(1)}, bf16[512,8,128]{0,2,1:T(8,128)(2,1)}, u32[]{:S(2)}) copy-start(bf16[512,8,128]{0,2,1:T(8,128)(2,1)} %copy.163) | copy-start | bytes 3145732
  166.7 2.3 copy-start.3
  166.7 2.3 copy-start.12
  166.7 2.5 copy-start.17
  169.7 1.3 copy-start.5
  173.1 4.4 %copy-start.4 = (bf16[8,512,512]{2,1,0:T(8,128)(2,1)S(1)}, bf16[8,512,512]{2,1,0:T(8,128)(2,1)}, u32[]{:S(2)}) copy-start(bf16[8,512,512]{2,1,0:T(8,128)(2,1)} %copy-done.3) | copy-start | bytes 12582916
  173.1 4.4 %copy-start.11 = (bf16[512,1024]{0,1:T(8,128)(2,1)S(1)}, bf16[512,1024]{0,1:T(8,128)(2,1)}, u32[]{:S(2)}) copy-start(bf16[512,1024]{0,1:T(8,128)(2,1)} %copy.213) | copy-start | bytes 3145732
  212.9 1.3 copy-start.6
  216.8 1.3 copy-start.7
  218.4 10.3 %collective-permute-start.1 = (f32[3,3,1024]{2,1,0:T(4,128)S(1)}, f32[3,3,1024]{2,1,0:T(4,128)S(1)}, u32[]{:S(2)}, u32[]{:S(2)}) collective-permute-start(f32[3,3,1024]{2,1,0:T(4,128)S(1)} %pad_maximum_fusion.3), channel_id=1, source_target_pairs={{2,0},{4,2},{6,4},{8,6},{10,8},{12,10},{14,12},{16,14},{18,16},{20... | collective-permute-start | bytes 110600 | tf_op jit(solution)/shard_map/ppermute | solution.py:16
  228.8 8.9 %copy-start.1 = (f32[515,1024]{1,0:T(8,128)S(1)}, f32[515,1024]{1,0:T(8,128)}, u32[]{:S(2)}) copy-start(f32[515,1024]{1,0:T(8,128)} %copy-done) | copy-start | bytes 6328324
  228.8 8.9 %copy-start.15 = (f32[512,1024]{1,0:T(8,128)S(1)}, f32[512,1024]{1,0:T(8,128)}, u32[]{:S(2)}) copy-start(f32[512,1024]{1,0:T(8,128)} %copy.176) | copy-start | bytes 6291460
  237.7 3.0 copy-start.14
Sparse Core Ops, SparseCore 0:
  27.6 77.4 all-gather.6
  144.1 48.9 all-gather.8
where the time goes:
time: 311 us; the launch traced here: 310 us
  blocking collectives  111 us (36%)
  other arithmetic  55.7 us (18%)
  waiting for transfers between devices  48.9 us (16%)
  matrix products  41.3 us (13%)
  local copies, waits for them, and re-layouts  34.1 us (11%)
  between operations  14.5 us (5%)
  starting transfers between devices  3.99 us (1%)
    psum x1, blocking collectives, body(): conv_grad, gain_grad = lax.psum((conv_part, gain_part), 'ctx')  59.3 us
    all_gather x1, waiting for transfers between devices, body(): lax.all_gather(device_sum[1][None], 'ctx', axis=0, tiled=True)  35.3 us
    all_gather x1, blocking collectives, body(): all_totals = lax.all_gather(device_sum[0][None], 'ctx', axis=0, tiled=True)  22.8 us
    all_gather x1, blocking collectives, prefix(): lax.all_gather(a.astype(kind), axis)  18.6 us
    add x15, other arithmetic, chain_step(): jnp.exp(later_part[0])[..., None, None] * earlier[1] + later_part[1]  16.6 us
    reduce_sum x3, other arithmetic, conv_backward(): jnp.sum(grad_rows * extended[TAPS - 1:TAPS - 1 + tok_here], axis=0)  14.7 us
    all_gather x1, waiting for transfers between devices, prefix(): lax.all_gather(a.astype(kind), axis)  13.5 us
    dot_general x1, matrix products, body(): jnp.einsum('nh,nhde->hde', factor_table, lax.all_gather(device_sum[1][Non...  12.5 us
  transfers between devices with their start and end apart: 4, of which 2 were waited for; matrix products, arithmetic and copies ran while one was open for 14% of the time, Pallas kernels for 0%

commit v1 on v0

--- a/solution.py
+++ b/solution.py
@@ -128,7 +128,14 @@
     )
     device_sum, before = local_chain(closing, blocks, False)
     zero_state = jnp.zeros((heads_here, HD, HD), jnp.float32)
-    all_totals = lax.all_gather(device_sum[0][None], "ctx", axis=0, tiled=True)
+    ways, here = (lax.axis_size("ctx"), lax.axis_index("ctx"))
+    all_totals, reach = (device_sum[0][None], 1)
+    while reach < ways:
+        theirs = lax.ppermute(all_totals, "ctx", [(d, d ^ reach) for d in range(ways)])
+        mine_first = jnp.concatenate([all_totals, theirs], axis=0)
+        theirs_first = jnp.concatenate([theirs, all_totals], axis=0)
+        all_totals = jnp.where(here & reach == 0, mine_first, theirs_first)
+        reach = 2 * reach
     device_index = lax.axis_index("ctx")
     cumulative = jnp.cumsum(all_totals, axis=0)
     before_me = cumulative[device_index] - all_totals[device_index]

time: 311 us -> 311 us (level)
  blocking collectives: 111 us -> 88 us
  waiting for transfers between devices: 48.9 us -> 63.6 us
  starting transfers between devices: 3.99 us -> 12.7 us
    all_gather x1 -> x0, blocking collectives: 22.8 us -> none  [body(): all_totals = lax.all_gather(device_sum[0][None], 'ctx', axis=0, tiled=True)]
    all_gather x1, waiting for transfers between devices: 35.3 us -> 43.9 us  [body(): lax.all_gather(device_sum[1][None], 'ctx', axis=0, tiled=True)]
    ppermute x0 -> x4, starting transfers between devices: none -> 8.51 us  [body(): lax.ppermute(all_totals, 'ctx', [(d, d ^ reach) for d in range(ways)])]
    ppermute x0 -> x4, waiting for transfers between devices: none -> 6.11 us  [body(): lax.ppermute(all_totals, 'ctx', [(d, d ^ reach) for d in range(ways)])]
    unnamed x3 -> x4, other arithmetic: 6.81 us -> 7.4 us
    another operation x8 -> x5, local copies, waits for them, and re-layouts: 6.37 us -> 6.04 us
    unnamed x61 -> x55, local copies, waits for them, and re-layouts: 8.88 us -> 8.84 us
  transfers between devices with their start and end apart: 4 -> 8, of which waited for: 2 -> 5; matrix products, arithmetic and copies ran while one was open for 14% -> 14% of each run, Pallas kernels for 0% -> 0%
where the time goes in v1:
time: 311 us; the launch traced here: 310 us
  blocking collectives  88 us (28%)
  waiting for transfers between devices  63.6 us (20%)
  other arithmetic  57.5 us (18%)
  matrix products  41.3 us (13%)
  local copies, waits for them, and re-layouts  32.1 us (10%)
  between operations  14.5 us (5%)
  starting transfers between devices  12.7 us (4%)
    psum x1, blocking collectives, body(): conv_grad, gain_grad = lax.psum((conv_part, gain_part), 'ctx')  59.3 us
    all_gather x1, waiting for transfers between devices, body(): lax.all_gather(device_sum[1][None], 'ctx', axis=0, tiled=True)  43.9 us
    all_gather x1, blocking collectives, prefix(): lax.all_gather(a.astype(kind), axis)  18.6 us
    add x15, other arithmetic, chain_step(): jnp.exp(later_part[0])[..., None, None] * earlier[1] + later_part[1]  16.6 us
    reduce_sum x3, other arithmetic, conv_backward(): jnp.sum(grad_rows * extended[TAPS - 1:TAPS - 1 + tok_here], axis=0)  14.7 us
    all_gather x1, waiting for transfers between devices, prefix(): lax.all_gather(a.astype(kind), axis)  13.6 us
    dot_general x1, matrix products, body(): jnp.einsum('nh,nhde->hde', factor_table, lax.all_gather(device_sum[1][Non...  12.5 us
    unnamed x55, local copies, waits for them, and re-layouts  8.84 us
  transfers between devices with their start and end apart: 8, of which 5 were waited for; matrix products, arithmetic and copies ran while one was open for 14% of the time, Pallas kernels for 0%

profile of v1, /device:TPU:0, one launch (start us, length us, event | category | flops | bytes accessed | tf_op | source)
XLA Modules:
  0.0 310.1 jit_solution(12968005588582216412)
XLA Ops:
  8.8 2.4 collective-permute-start
  11.2 2.2 reduce-window.6
  15.6 2.9 maximum_convert_fusion
  20.0 1.5 copy.153
  21.5 4.9 %fusion.49 = bf16[64,8,8,128]{3,2,1,0:T(8,128)(2,1)S(1)} fusion(f32[515,1024]{1,0:T(8,128)} %maximum_convert_fusion, f32[1024]{0:T(1024)S(1)} %bitcast.220, f32[1024]{0:T(1024)S(1)} %bitcast.222, f32[1024]{0:T(1024)S(1)} %bitcast.224, f32[1024]{0:T(1024)S(1)} %bitcast.218), kind=kLoop, calls=%fused_computation.94 | loop fusion | flops 4194304 | bytes 9453568
  28.0 2.7 collective-permute-start.1
  32.7 1.6 collective-permute-start.2
  34.2 2.0 collective-permute-done.2
  36.3 1.6 collective-permute-start.3
  37.9 2.0 collective-permute-done.3
  40.0 2.6 collective-permute-start.4
  42.6 2.1 collective-permute-done.4
  45.5 1.5 maximum_convert_fusion.1
  47.0 1.3 copy-done
  48.4 1.9 add_convert_fusion.1
  50.3 2.3 copy.200
  53.8 2.9 multiply_convert_fusion.1
  56.7 2.0 copy-done.2
  58.7 2.8 fusion.42
  61.5 43.9 %all-gather.6.cloned.1.call-done = f32[128,128,128]{2,1,0:T(8,128)} async-done(((f32[8,128,128]{2,1,0:T(8,128)}), f32[128,128,128]{2,1,0:T(8,128)}) %all-gather.6.cloned.1.call-update) | async-done | bytes 8388624 | tf_op jit(solution)/shard_map/all_gather | solution.py:151
  105.4 12.5 %fusion = f32[8,1,128,128]{3,1,2,0:T(1,128)S(1)} fusion(f32[16,8,1,1]{0,2,3,1:T(1,128)S(1)} %copy.194, f32[16,8,128,128]{3,2,1,0:T(8,128)} %bitcast.189), kind=kOutput, calls=%fused_computation.2 | convolution fusion | flops 25165824 | bytes 8913408 | tf_op jit(solution)/shard_map/nh,nhde->hde/dot_general | solution.py:148
  118.0 1.9 multiply_reduce_fusion.12
  119.8 5.1 %psum.28 = f32[512]{0:T(512)S(1)} all-reduce(f32[512]{0:T(512)S(1)} %get-tuple-element.206), channel_id=1, replica_groups=mesh['ctx'=16,'head'=2] {'head'}, use_global_device_ids=true, to_apply=%region_4.5 | all-reduce | flops 512 | bytes 4096 | tf_op jit(solution)/shard_map/psum | solution.py:167
  125.0 2.9 copy.157
  127.9 2.6 fusion.7
  130.5 4.9 %psum.29 = f32[512]{0:T(512)S(1)} all-reduce(f32[512]{0:T(512)S(1)} %get-tuple-element.166), channel_id=1, replica_groups=mesh['ctx'=16,'head'=2] {'head'}, use_global_device_ids=true, to_apply=%region_6.7 | all-reduce | flops 512 | bytes 4096 | tf_op jit(solution)/shard_map/psum | solution.py:169
  135.5 3.9 %fusion.6 = (bf16[512,1024]{1,0:T(8,128)(2,1)}, bf16[512,1024]{1,0:T(8,128)(2,1)}) fusion(bf16[512,1024]{1,0:T(8,128)(2,1)} %param.15, f32[512,1024]{1,0:T(8,128)} %copy.157, f32[512]{0:T(512)S(1)} %multiply_multiply_fusion, f32[1024]{0:T(1024)S(1)} %copy-done.22, f32[512]{0:T(512)S(1)} %add_rsqrt_fusion), kind=kLoop, calls=%fused_computation.19 | loop fusion | flops 4718592 | bytes 5251072 | tf_op jit(solution)/shard_map/convert_element_type | solution.py:43
  139.3 2.3 copy.201
  141.6 2.7 fusion.39
  144.3 18.6 %all-gather.2 = bf16[16,1,8]{2,1,0:T(2,128)(2,1)S(1)} all-gather(bf16[1,1,8]{2,1,0:T(2,128)(2,1)S(1)} %copy-done.24), channel_id=1, replica_groups=mesh['ctx'=16,'head'=2] {'ctx'}, dimensions={0}, use_global_device_ids=true | all-gather | bytes 272 | tf_op jit(solution)/shard_map/all_gather | solution.py:24
  163.0 4.0 %multiply_convert_fusion = bf16[8,512,512]{2,1,0:T(8,128)(2,1)S(1)} fusion(f32[8,512]{1,0:T(8,128)} %bitcast_add_fusion.1, pred[512,512]{1,0:T(8,128)(4,1)S(1)} %iota_compare_fusion, bf16[512,8,128]{0,2,1:T(8,128)(2,1)} %bitcast.186, bf16[64,8,8,128]{3,2,1,0:T(8,128)(2,1)S(1)} %fusion.49), kind=kOutput, calls=%fused_computation.4 | convolution fusion | flops 547356672 | bytes 6569984 | tf_op jit(solution)/shard_map/nthe,nshe->nhts/dot_general | solution.py:178
  167.0 1.5 fusion.61
  170.0 1.3 copy-done.5
  173.4 4.4 %fusion.63 = f32[8,128,512]{2,1,0:T(8,128)} fusion(bf16[512,8,128]{0,2,1:T(8,128)(2,1)S(1)} %bitcast.188, bf16[8,512,512]{2,1,0:T(8,128)(2,1)} %copy-done.2), kind=kOutput, calls=%fused_computation.142 | convolution fusion | flops 536870912 | bytes 7340032 | tf_op jit(solution)/shard_map/nhts,nthe->nshe/dot_general | solution.py:211
  177.8 2.0 fusion.62
  179.8 13.6 %all-gather.8.cloned.1.call-done = bf16[128,128,128]{2,1,0:T(8,128)(2,1)} async-done(((bf16[8,128,128]{2,1,0:T(8,128)(2,1)}), bf16[128,128,128]{2,1,0:T(8,128)(2,1)}) %all-gather.8.cloned.1.call-update) | async-done | bytes 4194320 | tf_op jit(solution)/shard_map/all_gather | solution.py:24
  193.4 17.3 %while.9 = (s32[]{:T(128)}, f32[8,128,128]{2,1,0:T(8,128)S(1)}, s32[]{:T(128)}, bf16[16,8]{1,0:T(8,128)(2,1)S(1)}, bf16[16,8,128,128]{3,2,1,0:T(8,128)(2,1)}, /*index=5*/s32[]{:T(128)}, s32[]{:T(128)}, s32[]{:T(128)}, s32[]{:T(128)}) while((s32[]{:T(128)}, f32[8,128,128]{2,1,0:T(8,128)S(1)}, s32[]{:T(128)}, bf16[16,8]{1,0:T(8,128)(2,1)S(1)}, ...), condition=%wide.region_8.9_spmd, body=%wide.region_7.8_spmd.sunk | while | flops 393230 | bytes 1310955 | solution.py:39
  210.7 2.4 fusion.35
  214.7 2.4 fusion.36
  217.1 1.3 copy-done.7
  218.7 1.6 collective-permute-start.5
  220.3 3.0 copy.164
  223.2 2.9 copy.180
  226.1 2.9 copy.178
  229.1 8.9 %multiply_reduce_fusion.3 = (f32[1024]{0:T(1024)S(1)}, f32[1024]{0:T(1024)S(1)}, f32[1024]{0:T(1024)S(1)}, f32[1024]{0:T(1024)S(1)}, bf16[512,1024]{1,0:T(8,128)(2,1)}) fusion(f32[512,1024]{1,0:T(8,128)} %copy.180, f32[515,1024]{1,0:T(8,128)} %maximum_convert_fusion, f32[3,1024]{1,0:T(4,128)S(1)} %get-tuple-element.186, f32[1024]{0:T(1024)S(1)} %bitcast.221, ...), kind=kLoop, calls=%fused_computation.62 | loop fusion | flops 9957376 | bytes 11579392 | tf_op jit(solution)/shard_map/reduce_sum | solution.py:86
  238.0 2.9 multiply_reduce_fusion.11
  240.9 2.9 multiply_reduce_fusion.7
  243.9 59.3 %all-reduce = (f32[3,4,1024]{2,1,0:T(4,128)}, f32[1024]{0:T(1024)}) all-reduce(f32[3,4,1024]{2,1,0:T(4,128)S(1)} %pad_maximum_fusion.4, f32[1024]{0:T(1024)S(1)} %get-tuple-element.165), channel_id=1, replica_groups=mesh['ctx'=16,'head'=2] {'ctx'}, use_global_device_ids=true, to_apply=%region_21.22 | all-reduce | flops 13312 | bytes 106496 | tf_op jit(solution)/shard_map/psum | solution.py:233
  (132 shorter events, 33.4 us)
Async XLA Ops:
  7.2 11.3 %copy-start.21 = (bf16[512,1024]{1,0:T(8,128)(2,1)S(1)}, bf16[512,1024]{1,0:T(8,128)(2,1)}, u32[]{:S(2)}) copy-start(bf16[512,1024]{1,0:T(8,128)(2,1)} %param.10) | copy-start | bytes 3145732
  7.2 98.3 %all-gather.6.cloned.1.call-start = ((), (), s32[]{:S(2)}) async-start(), calls=%async_computation | async-start | bytes 8912896 | tf_op jit(solution)/shard_map/all_gather | solution.py:151
  8.8 6.7 %collective-permute-start = (bf16[3,3,1024]{2,1,0:T(4,128)(2,1)S(1)}, bf16[3,3,1024]{2,1,0:T(4,128)(2,1)S(1)}, u32[]{:S(2)}, u32[]{:S(2)}) collective-permute-start(bf16[3,3,1024]{2,1,0:T(4,128)(2,1)S(1)} %pad_maximum_fusion.5), channel_id=1, source_target_pairs={{0,2},{2,4},{4,6},{6,8},{8,10},{10,12},{12,14},{14,16},{16,18},{18... | collective-permute-start | bytes 55304 | tf_op jit(solution)/shard_map/ppermute | solution.py:16
  15.5 10.9 %copy-start.25 = (f32[8]{0:T(128)}, f32[8]{0:T(128)S(1)}, u32[]{:S(2)}) copy-start(f32[8]{0:T(128)S(1)} %get-tuple-element.205) | copy-start | bytes 100
  21.5 4.9 %copy-start.18 = (bf16[512,8,128]{0,2,1:T(8,128)(2,1)S(1)}, bf16[512,8,128]{0,2,1:T(8,128)(2,1)}, u32[]{:S(2)}) copy-start(bf16[512,8,128]{0,2,1:T(8,128)(2,1)} %copy.153) | copy-start | bytes 3145732
  26.4 136.6 %copy-start.8 = (bf16[64,8,8,128]{3,2,1,0:T(8,128)(2,1)}, bf16[64,8,8,128]{3,2,1,0:T(8,128)(2,1)S(1)}, u32[]{:S(2)}) copy-start(bf16[64,8,8,128]{3,2,1,0:T(8,128)(2,1)S(1)} %fusion.49) | copy-start | bytes 3145732
  27.7 165.6 %all-gather.8.cloned.1.call-start = ((), (), s32[]{:S(2)}) async-start(), calls=%async_computation.1 | async-start | bytes 4456448 | tf_op jit(solution)/shard_map/all_gather | solution.py:24
  28.0 3.9 %collective-permute-start.1 = (f32[1,8]{1,0:T(1,128)S(1)}, f32[1,8]{1,0:T(1,128)}, u32[]{:S(2)}, u32[]{:S(2)}) collective-permute-start(f32[1,8]{1,0:T(1,128)S(1)} %bitcast.240), channel_id=1, source_target_pairs={{0,2},{2,0},{4,6},{6,4},{8,10},{10,8},{12,14},{14,12},{16,18},{18,... | collective-permute-start | bytes 104 | tf_op jit(solution)/shard_map/ppermute | solution.py:134
  32.7 3.6 %collective-permute-start.2 = (f32[2,8]{1,0:T(2,128)S(1)}, f32[2,8]{1,0:T(2,128)S(1)}, u32[]{:S(2)}, u32[]{:S(2)}) collective-permute-start(f32[2,8]{1,0:T(2,128)S(1)} %maximum_select_fusion.3), channel_id=1, source_target_pairs={{0,4},{2,6},{4,0},{6,2},{8,12},{10,14},{12,8},{14,10},{16,20},{18,... | collective-permute-start | bytes 200 | tf_op jit(solution)/shard_map/ppermute | solution.py:134
  36.3 3.7 %collective-permute-start.3 = (f32[4,8]{1,0:T(4,128)S(1)}, f32[4,8]{1,0:T(4,128)S(1)}, u32[]{:S(2)}, u32[]{:S(2)}) collective-permute-start(f32[4,8]{1,0:T(4,128)S(1)} %maximum_select_fusion.2), channel_id=1, source_target_pairs={{0,8},{2,10},{4,12},{6,14},{8,0},{10,2},{12,4},{14,6},{16,24},{18,... | collective-permute-start | bytes 392 | tf_op jit(solution)/shard_map/ppermute | solution.py:134
  40.0 4.7 %collective-permute-start.4 = (f32[8,8]{1,0:T(8,128)S(1)}, f32[8,8]{1,0:T(8,128)S(1)}, u32[]{:S(2)}, u32[]{:S(2)}) collective-permute-start(f32[8,8]{1,0:T(8,128)S(1)} %maximum_select_fusion.1), channel_id=1, source_target_pairs={{0,16},{2,18},{4,20},{6,22},{8,24},{10,26},{12,28},{14,30},{16,0},... | collective-permute-start | bytes 776 | tf_op jit(solution)/shard_map/ppermute | solution.py:134
  47.0 1.3 copy-start
  52.5 1.2 copy-start.9
  52.5 1.2 copy-start.23
  53.5 3.2 %copy-start.20 = (bf16[64,8,8,128]{3,2,1,0:T(8,128)(2,1)}, bf16[64,8,8,128]{3,2,1,0:T(8,128)(2,1)S(1)}, u32[]{:S(2)}) copy-start(bf16[64,8,8,128]{3,2,1,0:T(8,128)(2,1)S(1)} %fusion.77) | copy-start | bytes 3145732
  56.7 2.0 copy-start.2
  105.4 12.5 %copy-start.10 = (bf16[512,1024]{0,1:T(8,128)(2,1)S(1)}, bf16[512,1024]{0,1:T(8,128)(2,1)}, u32[]{:S(2)}) copy-start(bf16[512,1024]{0,1:T(8,128)(2,1)} %copy.200) | copy-start | bytes 3145732
  105.4 12.5 %copy-start.13 = (f32[8,128,512]{2,1,0:T(8,128)S(1)}, f32[8,128,512]{2,1,0:T(8,128)}, u32[]{:S(2)}) copy-start(f32[8,128,512]{2,1,0:T(8,128)} %fusion.42) | copy-start | bytes 6291460
  117.9 1.9 copy-start.16
  125.0 2.9 copy-start.22
  139.3 2.3 copy-start.26
  139.3 5.0 %copy-start.24 = (bf16[1,1,8]{2,1,0:T(2,128)(2,1)S(1)}, bf16[1,1,8]{2,1,0:T(2,128)(2,1)}, u32[]{:S(2)}) copy-start(bf16[1,1,8]{2,1,0:T(2,128)(2,1)} %get-tuple-element.204) | copy-start | bytes 52
  163.0 4.0 %copy-start.19 = (bf16[512,8,128]{0,2,1:T(8,128)(2,1)S(1)}, bf16[512,8,128]{0,2,1:T(8,128)(2,1)}, u32[]{:S(2)}) copy-start(bf16[512,8,128]{0,2,1:T(8,128)(2,1)} %copy.153) | copy-start | bytes 3145732
  167.0 2.3 copy-start.3
  167.0 2.3 copy-start.12
  167.0 2.5 copy-start.17
  170.0 1.3 copy-start.5
  173.4 4.4 %copy-start.4 = (bf16[8,512,512]{2,1,0:T(8,128)(2,1)S(1)}, bf16[8,512,512]{2,1,0:T(8,128)(2,1)}, u32[]{:S(2)}) copy-start(bf16[8,512,512]{2,1,0:T(8,128)(2,1)} %copy-done.3) | copy-start | bytes 12582916
  173.4 4.4 %copy-start.11 = (bf16[512,1024]{0,1:T(8,128)(2,1)S(1)}, bf16[512,1024]{0,1:T(8,128)(2,1)}, u32[]{:S(2)}) copy-start(bf16[512,1024]{0,1:T(8,128)(2,1)} %copy.200) | copy-start | bytes 3145732
  213.2 1.3 copy-start.6
  217.1 1.3 copy-start.7
  218.7 10.3 %collective-permute-start.5 = (f32[3,3,1024]{2,1,0:T(4,128)S(1)}, f32[3,3,1024]{2,1,0:T(4,128)S(1)}, u32[]{:S(2)}, u32[]{:S(2)}) collective-permute-start(f32[3,3,1024]{2,1,0:T(4,128)S(1)} %pad_maximum_fusion.3), channel_id=1, source_target_pairs={{2,0},{4,2},{6,4},{8,6},{10,8},{12,10},{14,12},{16,14},{18,16},{20... | collective-permute-start | bytes 110600 | tf_op jit(solution)/shard_map/ppermute | solution.py:16
  229.0 8.9 %copy-start.1 = (f32[515,1024]{1,0:T(8,128)S(1)}, f32[515,1024]{1,0:T(8,128)}, u32[]{:S(2)}) copy-start(f32[515,1024]{1,0:T(8,128)} %copy-done) | copy-start | bytes 6328324
  229.1 8.9 %copy-start.15 = (f32[512,1024]{1,0:T(8,128)S(1)}, f32[512,1024]{1,0:T(8,128)}, u32[]{:S(2)}) copy-start(f32[512,1024]{1,0:T(8,128)} %copy.164) | copy-start | bytes 6291460
  238.0 3.0 copy-start.14
Sparse Core Ops, SparseCore 0:
  27.9 77.5 all-gather.5
  144.4 48.9 all-gather.7
